TPU v7x, 256 devices: a whole 4x4x8 slice. The times are simulated.
256 devices in a mesh: section: 8 (over x, core), blk: 32 (over y, z).
Axes of the slice: x: 4, y: 4, z: 8, core: 2. Of those that a mesh axis runs over, the one named last changes fastest.
Arguments:
- hidden: bfloat16 [16384, 1536], P('blk'), may hold values from -6 to 6
- stale_kv: bfloat16 [8, 16384, 3072], P('section', 'blk'), may hold values from -6 to 6
- w_qkv: bfloat16 [8, 1536, 4608], P('section', 'blk'), may hold values from -0.15625 to 0.15625
- w_out: bfloat16 [8, 1536, 1536], P('section', 'blk'), may hold values from -0.15625 to 0.15625
- q_gain: float32 [8, 128], P('section'), may hold values from 0.25 to 1.75
- k_gain: float32 [8, 128], P('section'), may hold values from 0.25 to 1.75
- mod_table: float32 [8, 16, 3, 1536], P('section'), may hold values from -4 to 4
- pattern: int32 [128, 8], P('blk'), may hold values from 0 to 1, as said below
- step_index: int32 [128], P('blk'), may hold values from 0 to 15
- order: int32 [4], replicated, may hold values from 0 to 3, each once
Outputs:
- layer_out: bfloat16 [8, 16384, 1536], P('section', 'blk')
- kv_cache: bfloat16 [8, 16384, 3072], P('section', 'blk')
Inputs may be any that keep to these rules, and one draw needn't show every extreme that they name: `pattern`: every row of the query tile's own tile (candidate c = tile index mod 4) is 1. `order`: names each patch once.
All inputs are finite; a program needn't handle non-finite values.
Results may differ from a plain program's by a relative error of at most 0.01.
Values may be sent and summed in bfloat16 or wider, within the bound.
A program may use at most 128 MiB of HBM per device.

v0:
```python
import math
import jax
import jax.numpy as jnp
from jax import lax
from jax.sharding import PartitionSpec as P

D = 1536
HEADS = 12
HDIM = 128
TILE = 128
PATCHES = 4
TSTEPS = 16
TOK_DEV = 128
NORM_EPS = 1e-06


def shifted(value, axis, steps):
    count = lax.axis_size(axis)
    pairs = [(source, (source + steps) % count) for source in range(count)]
    return lax.ppermute(value, axis, pairs)


def shifted_2(x, axis, by):
    count = lax.axis_size(axis)
    pairs = [(i, i + by) for i in range(count) if 0 <= i + by < count]
    return lax.ppermute(x, axis, pairs)


def layer_norm(values):
    centre = values - jnp.mean(values, axis=-1, keepdims=True)
    spread = jnp.mean(centre * centre, axis=-1, keepdims=True)
    return centre * lax.rsqrt(spread + NORM_EPS)


def head_norm(values, gain_row):
    square = jnp.mean(values * values, axis=-1, keepdims=True)
    return values * lax.rsqrt(square + NORM_EPS) * gain_row


def on_device(
    hidden, stale_kv, w_qkv, w_out, q_gain, k_gain, mod_table, pattern, step_index, order
):
    inner_width = HEADS * HDIM
    rows_patch = TOK_DEV
    tiles_patch = rows_patch // TILE
    candidate_tiles = pattern.shape[1]
    sections = lax.axis_size("section")
    section_id = lax.axis_index("section")
    full_qkv, full_out = (
        lax.all_gather(w_qkv[0], "blk", axis=0, tiled=True),
        lax.all_gather(w_out[0], "blk", axis=0, tiled=True),
    )
    query_gain = q_gain[0]
    key_gain = k_gain[0]
    modulation_table = mod_table[0].reshape(TSTEPS, 3 * D)
    tile_masks = pattern.reshape(PATCHES, tiles_patch, candidate_tiles)
    steps_tiles = step_index.reshape(PATCHES, tiles_patch)
    input_rows = hidden.reshape(PATCHES, rows_patch, D)
    own_store = stale_kv[0].reshape(PATCHES, rows_patch, 2 * inner_width)
    near_store = shifted(own_store, "blk", 1)
    received = jnp.zeros((rows_patch, D), jnp.bfloat16)
    results = jnp.zeros((PATCHES, rows_patch, D), jnp.bfloat16)
    inverse_root = 1.0 / math.sqrt(HDIM)

    def slot_step(slot, state_now):
        received, own_store, near_store, results = state_now
        offset = slot - section_id
        active = jnp.logical_and(offset >= 0, offset < PATCHES)
        clipped = jnp.clip(offset, 0, PATCHES - 1)
        patch_id = jnp.sum(jnp.where(jnp.arange(PATCHES) == clipped, order, 0))
        tokens = jnp.where(
            section_id == 0,
            lax.dynamic_index_in_dim(input_rows, patch_id, 0, keepdims=False),
            received,
        )
        tile_steps = lax.dynamic_index_in_dim(steps_tiles, patch_id, 0, keepdims=False)
        one_hot = (tile_steps[:, None] == jnp.arange(TSTEPS)[None, :]).astype(jnp.float32)
        modulation = jnp.dot(one_hot, modulation_table, precision=lax.Precision.HIGHEST)
        modulation = jnp.broadcast_to(modulation[:, None, :], (tiles_patch, TILE, 3 * D)).reshape(
            rows_patch, 3 * D
        )
        shift_term = modulation[:, :D]
        scale_term = modulation[:, D : 2 * D]
        gate_term = modulation[:, 2 * D :]

        def project(token_rows):
            modulated = (
                layer_norm(token_rows.astype(jnp.float32)) * (1.0 + scale_term) + shift_term
            ).astype(jnp.bfloat16)
            qkv = jnp.dot(modulated, full_qkv, preferred_element_type=jnp.float32)
            queries = head_norm(
                qkv[:, :inner_width].reshape(rows_patch, HEADS, HDIM), query_gain
            ).astype(jnp.bfloat16)
            return (modulated, queries, qkv[:, inner_width:].astype(jnp.bfloat16))

        def spare_project(token_rows):
            return (
                jnp.zeros((rows_patch, D), jnp.bfloat16),
                jnp.zeros((rows_patch, HEADS, HDIM), jnp.bfloat16),
                jnp.zeros((rows_patch, 2 * inner_width), jnp.bfloat16),
            )

        modulated, queries, fresh_kv = lax.cond(active, project, spare_project, tokens)
        own_store = jnp.where(
            active, lax.dynamic_update_index_in_dim(own_store, fresh_kv, patch_id, 0), own_store
        )
        near_fresh = shifted(fresh_kv, "blk", 1)
        near_store = jnp.where(
            active, lax.dynamic_update_index_in_dim(near_store, near_fresh, patch_id, 0), near_store
        )
        tile_mask = lax.dynamic_index_in_dim(tile_masks, patch_id, 0, keepdims=False)

        def attend(operands):
            token_rows, query_rows, own_rows, near_rows = operands
            candidates = jnp.concatenate(
                [own_rows.reshape(-1, 2 * inner_width), near_rows.reshape(-1, 2 * inner_width)],
                axis=0,
            )
            key_rows = head_norm(
                candidates[:, :inner_width].astype(jnp.float32).reshape(-1, HEADS, HDIM), key_gain
            ).astype(jnp.bfloat16)
            value_rows = candidates[:, inner_width:].reshape(-1, HEADS, HDIM)
            token_mask = jnp.broadcast_to(
                tile_mask.astype(jnp.float32)[:, None, :, None],
                (tiles_patch, TILE, candidate_tiles, TILE),
            ).reshape(rows_patch, candidate_tiles * TILE)
            scores = (
                jnp.einsum("qhd,khd->hqk", query_rows, key_rows, preferred_element_type=jnp.float32)
                * inverse_root
            )
            expo = jnp.exp(scores) * token_mask[None]
            weight_sum = jnp.sum(expo, axis=-1)
            mixture = jnp.einsum(
                "hqk,khd->qhd",
                expo.astype(jnp.bfloat16),
                value_rows,
                preferred_element_type=jnp.float32,
            )
            attended = (
                (mixture / jnp.transpose(weight_sum)[:, :, None])
                .reshape(rows_patch, inner_width)
                .astype(jnp.bfloat16)
            )
            projected = jnp.dot(attended, full_out, preferred_element_type=jnp.float32)
            return (token_rows.astype(jnp.float32) + gate_term * projected).astype(jnp.bfloat16)

        def spare_attend(operands):
            return jnp.zeros((rows_patch, D), jnp.bfloat16)

        output_rows = lax.cond(
            active, attend, spare_attend, (tokens, queries, own_store, near_store)
        )
        results = jnp.where(
            active, lax.dynamic_update_index_in_dim(results, output_rows, patch_id, 0), results
        )
        received = shifted_2(output_rows, "section", 1)
        return (received, own_store, near_store, results)

    slot_count = PATCHES + sections - 1
    received, own_store, near_store, results = lax.fori_loop(
        0, slot_count, slot_step, (received, own_store, near_store, results)
    )
    layer_out = results.reshape(1, PATCHES * rows_patch, D)
    kv_cache = own_store.reshape(1, PATCHES * rows_patch, 2 * inner_width)
    return (layer_out, kv_cache)


def solution(mesh):
    in_specs = (
        P("blk", None),
        P("section", "blk", None),
        P("section", "blk", None),
        P("section", "blk", None),
        P("section", None),
        P("section", None),
        P("section", None, None, None),
        P("blk", None),
        P("blk"),
        P(),
    )
    out_specs = (P("section", "blk", None), P("section", "blk", None))
    return jax.shard_map(
        on_device, mesh=mesh, in_specs=in_specs, out_specs=out_specs, check_vma=False
    )
```

profile of v0, /device:TPU:7, one launch (start us, length us, event | category | flops | bytes accessed | tf_op | source)
XLA Modules:
  0.0 1030.1 jit_solution(15740919164373035649)
XLA Ops:
  7.2 3.8 copy.63
  14.6 101.2 %collective-permute-done.2 = bf16[4,128,3072]{2,1,0:T(8,128)(2,1)} collective-permute-done((bf16[4,128,3072]{2,1,0:T(8,128)(2,1)}, bf16[4,128,3072]{2,1,0:T(8,128)(2,1)}, u32[]{:S(2)}, u32[]{:S(2)}) %collective-permute-start.2) | collective-permute-done | bytes 3145760 | tf_op jit(solution)/shard_map/ppermute | solution.py:20
  115.7 125.9 %all-gather.5.cloned.1.call-done = bf16[1,1536,4608]{2,1,0:T(8,128)(2,1)} async-done(((bf16[1,48,4608]{2,1,0:T(8,128)(2,1)}), bf16[1,1536,4608]{2,1,0:T(8,128)(2,1)}) %all-gather.5.cloned.1.call-update) | async-done | bytes 14155792 | tf_op jit(solution)/shard_map/all_gather | solution.py:50
  242.9 780.4 %while.20 = (s32[]{:T(128)}, bf16[128,1536]{1,0:T(8,128)(2,1)S(1)}, bf16[4,128,3072]{2,1,0:T(8,128)(2,1)}, bf16[4,128,3072]{2,1,0:T(8,128)(2,1)}, bf16[4,128,153...) while((s32[]{:T(128)}, bf16[128,1536]{1,0:T(8,128)(2,1)S(1)}, ...), condition=%wide.region_11.12_spmd, body=%wide.region_0.11_spmd.sunk | while | flops 3260855808 | bytes 107183792 | solution.py:160
  254.6 19.3 %collective-permute-done = bf16[128,3072]{1,0:T(8,128)(2,1)S(1)} collective-permute-done((bf16[128,3072]{1,0:T(8,128)(2,1)}, bf16[128,3072]{1,0:T(8,128)(2,1)S(1)}, u32[]{:S(2)}, u32[]{:S(2)}) %collective-permute-start) | collective-permute-done | bytes 786464 | tf_op jit(solution)/shard_map/while/body/eval_jaxpr/ppermute | solution.py:20
  294.6 14.4 %collective-permute-done = bf16[128,3072]{1,0:T(8,128)(2,1)S(1)} collective-permute-done((bf16[128,3072]{1,0:T(8,128)(2,1)}, bf16[128,3072]{1,0:T(8,128)(2,1)S(1)}, u32[]{:S(2)}, u32[]{:S(2)}) %collective-permute-start) | collective-permute-done | bytes 786464 | tf_op jit(solution)/shard_map/while/body/eval_jaxpr/ppermute | solution.py:20
  315.9 7.1 collective-permute-done.1
  334.6 13.3 %collective-permute-done = bf16[128,3072]{1,0:T(8,128)(2,1)S(1)} collective-permute-done((bf16[128,3072]{1,0:T(8,128)(2,1)}, bf16[128,3072]{1,0:T(8,128)(2,1)S(1)}, u32[]{:S(2)}, u32[]{:S(2)}) %collective-permute-start) | collective-permute-done | bytes 786464 | tf_op jit(solution)/shard_map/while/body/eval_jaxpr/ppermute | solution.py:20
  354.8 8.2 collective-permute-done.1
  374.6 14.4 %collective-permute-done = bf16[128,3072]{1,0:T(8,128)(2,1)S(1)} collective-permute-done((bf16[128,3072]{1,0:T(8,128)(2,1)}, bf16[128,3072]{1,0:T(8,128)(2,1)S(1)}, u32[]{:S(2)}, u32[]{:S(2)}) %collective-permute-start) | collective-permute-done | bytes 786464 | tf_op jit(solution)/shard_map/while/body/eval_jaxpr/ppermute | solution.py:20
  395.9 7.1 collective-permute-done.1
  414.6 14.4 %collective-permute-done = bf16[128,3072]{1,0:T(8,128)(2,1)S(1)} collective-permute-done((bf16[128,3072]{1,0:T(8,128)(2,1)}, bf16[128,3072]{1,0:T(8,128)(2,1)S(1)}, u32[]{:S(2)}, u32[]{:S(2)}) %collective-permute-start) | collective-permute-done | bytes 786464 | tf_op jit(solution)/shard_map/while/body/eval_jaxpr/ppermute | solution.py:20
  435.9 7.1 collective-permute-done.1
  454.6 14.4 %collective-permute-done = bf16[128,3072]{1,0:T(8,128)(2,1)S(1)} collective-permute-done((bf16[128,3072]{1,0:T(8,128)(2,1)}, bf16[128,3072]{1,0:T(8,128)(2,1)S(1)}, u32[]{:S(2)}, u32[]{:S(2)}) %collective-permute-start) | collective-permute-done | bytes 786464 | tf_op jit(solution)/shard_map/while/body/eval_jaxpr/ppermute | solution.py:20
  475.9 7.1 collective-permute-done.1
  494.6 12.2 %collective-permute-done = bf16[128,3072]{1,0:T(8,128)(2,1)S(1)} collective-permute-done((bf16[128,3072]{1,0:T(8,128)(2,1)}, bf16[128,3072]{1,0:T(8,128)(2,1)S(1)}, u32[]{:S(2)}, u32[]{:S(2)}) %collective-permute-start) | collective-permute-done | bytes 786464 | tf_op jit(solution)/shard_map/while/body/eval_jaxpr/ppermute | solution.py:20
  513.7 209.5 %collective-permute-done.1 = bf16[128,1536]{1,0:T(8,128)(2,1)S(1)} collective-permute-done((bf16[128,1536]{1,0:T(8,128)(2,1)}, bf16[128,1536]{1,0:T(8,128)(2,1)S(1)}, u32[]{:S(2)}, u32[]{:S(2)}) %collective-permute-start.1) | collective-permute-done | bytes 393248 | tf_op jit(solution)/shard_map/while/body/eval_jaxpr/ppermute | solution.py:26
  729.7 13.7 %conditional.4 = (bf16[128,12,128]{0,2,1:T(8,128)(2,1)}, bf16[128,3072]{1,0:T(8,128)(2,1)}, bf16[1,128,3072]{2,1,0:T(8,128)(2,1)}) conditional(s32[]{:T(128)} %convert_element_type.92, () %tuple.70, (bf16[128,1536]{1,0:T(8,128)(2,1)S(1)}, f32[4608]{0:T(1024)}, bf16[1536,4608]{1,0:T(8,128)(2,1)}, f32[1,128]{1,0:T(1,128)S(1)}) %tuple.71), branch_computations={%region_2.2_spmd, %region_3.6_spmd} | conditional | flops 1815284864 | bytes 26018840 | solution.py:103
  730.9 7.1 fusion.6
  745.9 11.9 %collective-permute-done = bf16[128,3072]{1,0:T(8,128)(2,1)S(1)} collective-permute-done((bf16[128,3072]{1,0:T(8,128)(2,1)}, bf16[128,3072]{1,0:T(8,128)(2,1)S(1)}, u32[]{:S(2)}, u32[]{:S(2)}) %collective-permute-start) | collective-permute-done | bytes 786464 | tf_op jit(solution)/shard_map/while/body/eval_jaxpr/ppermute | solution.py:20
  760.1 24.4 %conditional.5 = (bf16[128,1536]{1,0:T(8,128)(2,1)}, bf16[1,128,1536]{2,1,0:T(8,128)(2,1)}) conditional(s32[]{:T(128)} %convert_element_type.92, () %tuple.69, (bf16[128,1536]{1,0:T(8,128)(2,1)S(1)}, f32[4608]{0:T(1024)}, bf16[4,128,3072]{2,1,0:T(8,128)(2,1)}, bf16[4,128,3072]{2,1,0:T(8,128)(2,1)}, f32[1,128]{1,0:T(1,128)S(1)}, ...), branch_computations={%region_7.7_spmd, %region_8.10_spmd} | conditional | flops 1443506688 | bytes 69053088 | solution.py:150
  763.3 4.7 copy.31
  768.0 5.6 pad_maximum_fusion
  775.2 3.3 bitcast_reduce_fusion
  787.7 10.2 collective-permute-done.1
  804.5 13.7 %conditional.4 = (bf16[128,12,128]{0,2,1:T(8,128)(2,1)}, bf16[128,3072]{1,0:T(8,128)(2,1)}, bf16[1,128,3072]{2,1,0:T(8,128)(2,1)}) conditional(s32[]{:T(128)} %convert_element_type.92, () %tuple.70, (bf16[128,1536]{1,0:T(8,128)(2,1)S(1)}, f32[4608]{0:T(1024)}, bf16[1536,4608]{1,0:T(8,128)(2,1)}, f32[1,128]{1,0:T(1,128)S(1)}) %tuple.71), branch_computations={%region_2.2_spmd, %region_3.6_spmd} | conditional | flops 1815284864 | bytes 26018840 | solution.py:103
  805.7 7.1 fusion.6
  820.7 11.9 %collective-permute-done = bf16[128,3072]{1,0:T(8,128)(2,1)S(1)} collective-permute-done((bf16[128,3072]{1,0:T(8,128)(2,1)}, bf16[128,3072]{1,0:T(8,128)(2,1)S(1)}, u32[]{:S(2)}, u32[]{:S(2)}) %collective-permute-start) | collective-permute-done | bytes 786464 | tf_op jit(solution)/shard_map/while/body/eval_jaxpr/ppermute | solution.py:20
  834.8 24.4 %conditional.5 = (bf16[128,1536]{1,0:T(8,128)(2,1)}, bf16[1,128,1536]{2,1,0:T(8,128)(2,1)}) conditional(s32[]{:T(128)} %convert_element_type.92, () %tuple.69, (bf16[128,1536]{1,0:T(8,128)(2,1)S(1)}, f32[4608]{0:T(1024)}, bf16[4,128,3072]{2,1,0:T(8,128)(2,1)}, bf16[4,128,3072]{2,1,0:T(8,128)(2,1)}, f32[1,128]{1,0:T(1,128)S(1)}, ...), branch_computations={%region_7.7_spmd, %region_8.10_spmd} | conditional | flops 1443506688 | bytes 69053088 | solution.py:150
  838.0 4.7 copy.31
  842.8 5.6 pad_maximum_fusion
  849.9 3.3 bitcast_reduce_fusion
  862.5 12.3 %collective-permute-done.1 = bf16[128,1536]{1,0:T(8,128)(2,1)S(1)} collective-permute-done((bf16[128,1536]{1,0:T(8,128)(2,1)}, bf16[128,1536]{1,0:T(8,128)(2,1)S(1)}, u32[]{:S(2)}, u32[]{:S(2)}) %collective-permute-start.1) | collective-permute-done | bytes 393248 | tf_op jit(solution)/shard_map/while/body/eval_jaxpr/ppermute | solution.py:26
  881.4 13.7 %conditional.4 = (bf16[128,12,128]{0,2,1:T(8,128)(2,1)}, bf16[128,3072]{1,0:T(8,128)(2,1)}, bf16[1,128,3072]{2,1,0:T(8,128)(2,1)}) conditional(s32[]{:T(128)} %convert_element_type.92, () %tuple.70, (bf16[128,1536]{1,0:T(8,128)(2,1)S(1)}, f32[4608]{0:T(1024)}, bf16[1536,4608]{1,0:T(8,128)(2,1)}, f32[1,128]{1,0:T(1,128)S(1)}) %tuple.71), branch_computations={%region_2.2_spmd, %region_3.6_spmd} | conditional | flops 1815284864 | bytes 26018840 | solution.py:103
  882.6 7.2 fusion.6
  897.6 11.9 %collective-permute-done = bf16[128,3072]{1,0:T(8,128)(2,1)S(1)} collective-permute-done((bf16[128,3072]{1,0:T(8,128)(2,1)}, bf16[128,3072]{1,0:T(8,128)(2,1)S(1)}, u32[]{:S(2)}, u32[]{:S(2)}) %collective-permute-start) | collective-permute-done | bytes 786464 | tf_op jit(solution)/shard_map/while/body/eval_jaxpr/ppermute | solution.py:20
  911.7 24.4 %conditional.5 = (bf16[128,1536]{1,0:T(8,128)(2,1)}, bf16[1,128,1536]{2,1,0:T(8,128)(2,1)}) conditional(s32[]{:T(128)} %convert_element_type.92, () %tuple.69, (bf16[128,1536]{1,0:T(8,128)(2,1)S(1)}, f32[4608]{0:T(1024)}, bf16[4,128,3072]{2,1,0:T(8,128)(2,1)}, bf16[4,128,3072]{2,1,0:T(8,128)(2,1)}, f32[1,128]{1,0:T(1,128)S(1)}, ...), branch_computations={%region_7.7_spmd, %region_8.10_spmd} | conditional | flops 1443506688 | bytes 69053088 | solution.py:150
  914.9 4.7 copy.31
  919.7 5.6 pad_maximum_fusion
  926.8 3.3 bitcast_reduce_fusion
  939.4 14.8 %collective-permute-done.1 = bf16[128,1536]{1,0:T(8,128)(2,1)S(1)} collective-permute-done((bf16[128,1536]{1,0:T(8,128)(2,1)}, bf16[128,1536]{1,0:T(8,128)(2,1)S(1)}, u32[]{:S(2)}, u32[]{:S(2)}) %collective-permute-start.1) | collective-permute-done | bytes 393248 | tf_op jit(solution)/shard_map/while/body/eval_jaxpr/ppermute | solution.py:26
  960.8 13.7 %conditional.4 = (bf16[128,12,128]{0,2,1:T(8,128)(2,1)}, bf16[128,3072]{1,0:T(8,128)(2,1)}, bf16[1,128,3072]{2,1,0:T(8,128)(2,1)}) conditional(s32[]{:T(128)} %convert_element_type.92, () %tuple.70, (bf16[128,1536]{1,0:T(8,128)(2,1)S(1)}, f32[4608]{0:T(1024)}, bf16[1536,4608]{1,0:T(8,128)(2,1)}, f32[1,128]{1,0:T(1,128)S(1)}) %tuple.71), branch_computations={%region_2.2_spmd, %region_3.6_spmd} | conditional | flops 1815284864 | bytes 26018840 | solution.py:103
  962.0 7.1 fusion.6
  977.0 15.9 %collective-permute-done = bf16[128,3072]{1,0:T(8,128)(2,1)S(1)} collective-permute-done((bf16[128,3072]{1,0:T(8,128)(2,1)}, bf16[128,3072]{1,0:T(8,128)(2,1)S(1)}, u32[]{:S(2)}, u32[]{:S(2)}) %collective-permute-start) | collective-permute-done | bytes 786464 | tf_op jit(solution)/shard_map/while/body/eval_jaxpr/ppermute | solution.py:20
  995.1 24.4 %conditional.5 = (bf16[128,1536]{1,0:T(8,128)(2,1)}, bf16[1,128,1536]{2,1,0:T(8,128)(2,1)}) conditional(s32[]{:T(128)} %convert_element_type.92, () %tuple.69, (bf16[128,1536]{1,0:T(8,128)(2,1)S(1)}, f32[4608]{0:T(1024)}, bf16[4,128,3072]{2,1,0:T(8,128)(2,1)}, bf16[4,128,3072]{2,1,0:T(8,128)(2,1)}, f32[1,128]{1,0:T(1,128)S(1)}, ...), branch_computations={%region_7.7_spmd, %region_8.10_spmd} | conditional | flops 1443506688 | bytes 69053088 | solution.py:150
  998.3 4.7 copy.31
  1003.0 5.6 pad_maximum_fusion
  1010.1 3.3 bitcast_reduce_fusion
  (274 shorter events, 274.5 us)
Async XLA Ops:
  7.2 6.4 copy-start
  7.2 108.6 %all-gather.7.cloned.1.call-start = ((), (), s32[]{:S(2)}) async-start(), calls=%async_computation.1 | async-start | bytes 4866048 | tf_op jit(solution)/shard_map/all_gather | solution.py:51
  11.0 231.9 %copy-start.1 = (f32[1,128]{1,0:T(1,128)S(1)}, f32[1,128]{1,0:T(1,128)}, u32[]{:S(2)}) copy-start(f32[1,128]{1,0:T(1,128)} %param.20) | copy-start | bytes 1540
  11.0 231.9 %copy-start.2 = (s32[4]{0:T(128)S(1)}, s32[4]{0:T(128)}, u32[]{:S(2)}) copy-start(s32[4]{0:T(128)} %param.25) | copy-start | bytes 52
  11.0 231.9 %copy-start.3 = (s32[4]{0:T(128)S(1)}, s32[4]{0:T(128)}, u32[]{:S(2)}) copy-start(s32[4]{0:T(128)} %param.24) | copy-start | bytes 52
  11.0 231.9 %copy-start.4 = (f32[1,128]{1,0:T(1,128)S(1)}, f32[1,128]{1,0:T(1,128)}, u32[]{:S(2)}) copy-start(f32[1,128]{1,0:T(1,128)} %param.21) | copy-start | bytes 1540
  11.0 230.5 %all-gather.5.cloned.1.call-start = ((), (), s32[]{:S(2)}) async-start(), calls=%async_computation | async-start | bytes 14598144 | tf_op jit(solution)/shard_map/all_gather | solution.py:50
  11.8 103.9 %collective-permute-start.2 = (bf16[4,128,3072]{2,1,0:T(8,128)(2,1)}, bf16[4,128,3072]{2,1,0:T(8,128)(2,1)}, u32[]{:S(2)}, u32[]{:S(2)}) collective-permute-start(bf16[4,128,3072]{2,1,0:T(8,128)(2,1)} %bitcast.20), channel_id=1, source_target_pairs={{0,1},{1,2},{2,3},{3,4},{4,5},{5,6},{6,7},{7,8},{8,9},{9,10},{10,1... | collective-permute-start | bytes 9437192 | tf_op jit(solution)/shard_map/ppermute | solution.py:20
  252.4 21.5 %collective-permute-start = (bf16[128,3072]{1,0:T(8,128)(2,1)}, bf16[128,3072]{1,0:T(8,128)(2,1)S(1)}, u32[]{:S(2)}, u32[]{:S(2)}) collective-permute-start(bf16[128,3072]{1,0:T(8,128)(2,1)} %get-tuple-element.585), channel_id=1, source_target_pairs={{0,1},{1,2},{2,3},{3,4},{4,5},{5,6},{6,7},{7,8},{8,9},{9,10},{10,1... | collective-permute-start | bytes 2359304 | tf_op jit(solution)/shard_map/while/body/eval_jaxpr/ppermute | solution.py:20
  277.7 5.3 collective-permute-start.1
  292.4 16.6 %collective-permute-start = (bf16[128,3072]{1,0:T(8,128)(2,1)}, bf16[128,3072]{1,0:T(8,128)(2,1)S(1)}, u32[]{:S(2)}, u32[]{:S(2)}) collective-permute-start(bf16[128,3072]{1,0:T(8,128)(2,1)} %get-tuple-element.585), channel_id=1, source_target_pairs={{0,1},{1,2},{2,3},{3,4},{4,5},{5,6},{6,7},{7,8},{8,9},{9,10},{10,1... | collective-permute-start | bytes 2359304 | tf_op jit(solution)/shard_map/while/body/eval_jaxpr/ppermute | solution.py:20
  312.7 10.2 collective-permute-start.1
  332.4 15.5 %collective-permute-start = (bf16[128,3072]{1,0:T(8,128)(2,1)}, bf16[128,3072]{1,0:T(8,128)(2,1)S(1)}, u32[]{:S(2)}, u32[]{:S(2)}) collective-permute-start(bf16[128,3072]{1,0:T(8,128)(2,1)} %get-tuple-element.585), channel_id=1, source_target_pairs={{0,1},{1,2},{2,3},{3,4},{4,5},{5,6},{6,7},{7,8},{8,9},{9,10},{10,1... | collective-permute-start | bytes 2359304 | tf_op jit(solution)/shard_map/while/body/eval_jaxpr/ppermute | solution.py:20
  351.6 11.3 %collective-permute-start.1 = (bf16[128,1536]{1,0:T(8,128)(2,1)}, bf16[128,1536]{1,0:T(8,128)(2,1)S(1)}, u32[]{:S(2)}, u32[]{:S(2)}) collective-permute-start(bf16[128,1536]{1,0:T(8,128)(2,1)} %get-tuple-element.587), channel_id=1, source_target_pairs={{0,32},{32,64},{64,96},{96,128},{128,160},{160,192},{192,224},{1,3... | collective-permute-start | bytes 1179656 | tf_op jit(solution)/shard_map/while/body/eval_jaxpr/ppermute | solution.py:26
  372.4 16.6 %collective-permute-start = (bf16[128,3072]{1,0:T(8,128)(2,1)}, bf16[128,3072]{1,0:T(8,128)(2,1)S(1)}, u32[]{:S(2)}, u32[]{:S(2)}) collective-permute-start(bf16[128,3072]{1,0:T(8,128)(2,1)} %get-tuple-element.585), channel_id=1, source_target_pairs={{0,1},{1,2},{2,3},{3,4},{4,5},{5,6},{6,7},{7,8},{8,9},{9,10},{10,1... | collective-permute-start | bytes 2359304 | tf_op jit(solution)/shard_map/while/body/eval_jaxpr/ppermute | solution.py:20
  392.7 10.2 collective-permute-start.1
  412.4 16.6 %collective-permute-start = (bf16[128,3072]{1,0:T(8,128)(2,1)}, bf16[128,3072]{1,0:T(8,128)(2,1)S(1)}, u32[]{:S(2)}, u32[]{:S(2)}) collective-permute-start(bf16[128,3072]{1,0:T(8,128)(2,1)} %get-tuple-element.585), channel_id=1, source_target_pairs={{0,1},{1,2},{2,3},{3,4},{4,5},{5,6},{6,7},{7,8},{8,9},{9,10},{10,1... | collective-permute-start | bytes 2359304 | tf_op jit(solution)/shard_map/while/body/eval_jaxpr/ppermute | solution.py:20
  432.7 10.2 collective-permute-start.1
  452.4 16.6 %collective-permute-start = (bf16[128,3072]{1,0:T(8,128)(2,1)}, bf16[128,3072]{1,0:T(8,128)(2,1)S(1)}, u32[]{:S(2)}, u32[]{:S(2)}) collective-permute-start(bf16[128,3072]{1,0:T(8,128)(2,1)} %get-tuple-element.585), channel_id=1, source_target_pairs={{0,1},{1,2},{2,3},{3,4},{4,5},{5,6},{6,7},{7,8},{8,9},{9,10},{10,1... | collective-permute-start | bytes 2359304 | tf_op jit(solution)/shard_map/while/body/eval_jaxpr/ppermute | solution.py:20
  472.7 10.2 collective-permute-start.1
  492.4 14.4 %collective-permute-start = (bf16[128,3072]{1,0:T(8,128)(2,1)}, bf16[128,3072]{1,0:T(8,128)(2,1)S(1)}, u32[]{:S(2)}, u32[]{:S(2)}) collective-permute-start(bf16[128,3072]{1,0:T(8,128)(2,1)} %get-tuple-element.585), channel_id=1, source_target_pairs={{0,1},{1,2},{2,3},{3,4},{4,5},{5,6},{6,7},{7,8},{8,9},{9,10},{10,1... | collective-permute-start | bytes 2359304 | tf_op jit(solution)/shard_map/while/body/eval_jaxpr/ppermute | solution.py:20
  510.5 212.6 %collective-permute-start.1 = (bf16[128,1536]{1,0:T(8,128)(2,1)}, bf16[128,1536]{1,0:T(8,128)(2,1)S(1)}, u32[]{:S(2)}, u32[]{:S(2)}) collective-permute-start(bf16[128,1536]{1,0:T(8,128)(2,1)} %get-tuple-element.587), channel_id=1, source_target_pairs={{0,32},{32,64},{64,96},{96,128},{128,160},{160,192},{192,224},{1,3... | collective-permute-start | bytes 1179656 | tf_op jit(solution)/shard_map/while/body/eval_jaxpr/ppermute | solution.py:26
  743.5 14.4 %collective-permute-start = (bf16[128,3072]{1,0:T(8,128)(2,1)}, bf16[128,3072]{1,0:T(8,128)(2,1)S(1)}, u32[]{:S(2)}, u32[]{:S(2)}) collective-permute-start(bf16[128,3072]{1,0:T(8,128)(2,1)} %get-tuple-element.585), channel_id=1, source_target_pairs={{0,1},{1,2},{2,3},{3,4},{4,5},{5,6},{6,7},{7,8},{8,9},{9,10},{10,1... | collective-permute-start | bytes 2359304 | tf_op jit(solution)/shard_map/while/body/eval_jaxpr/ppermute | solution.py:20
  775.1 6.0 slice-start
  778.5 2.7 slice-start.1
  784.5 13.5 %collective-permute-start.1 = (bf16[128,1536]{1,0:T(8,128)(2,1)}, bf16[128,1536]{1,0:T(8,128)(2,1)S(1)}, u32[]{:S(2)}, u32[]{:S(2)}) collective-permute-start(bf16[128,1536]{1,0:T(8,128)(2,1)} %get-tuple-element.587), channel_id=1, source_target_pairs={{0,32},{32,64},{64,96},{96,128},{128,160},{160,192},{192,224},{1,3... | collective-permute-start | bytes 1179656 | tf_op jit(solution)/shard_map/while/body/eval_jaxpr/ppermute | solution.py:26
  818.3 14.4 %collective-permute-start = (bf16[128,3072]{1,0:T(8,128)(2,1)}, bf16[128,3072]{1,0:T(8,128)(2,1)S(1)}, u32[]{:S(2)}, u32[]{:S(2)}) collective-permute-start(bf16[128,3072]{1,0:T(8,128)(2,1)} %get-tuple-element.585), channel_id=1, source_target_pairs={{0,1},{1,2},{2,3},{3,4},{4,5},{5,6},{6,7},{7,8},{8,9},{9,10},{10,1... | collective-permute-start | bytes 2359304 | tf_op jit(solution)/shard_map/while/body/eval_jaxpr/ppermute | solution.py:20
  849.9 6.0 slice-start
  853.2 2.7 slice-start.1
  859.3 15.6 %collective-permute-start.1 = (bf16[128,1536]{1,0:T(8,128)(2,1)}, bf16[128,1536]{1,0:T(8,128)(2,1)S(1)}, u32[]{:S(2)}, u32[]{:S(2)}) collective-permute-start(bf16[128,1536]{1,0:T(8,128)(2,1)} %get-tuple-element.587), channel_id=1, source_target_pairs={{0,32},{32,64},{64,96},{96,128},{128,160},{160,192},{192,224},{1,3... | collective-permute-start | bytes 1179656 | tf_op jit(solution)/shard_map/while/body/eval_jaxpr/ppermute | solution.py:26
  895.2 14.4 %collective-permute-start = (bf16[128,3072]{1,0:T(8,128)(2,1)}, bf16[128,3072]{1,0:T(8,128)(2,1)S(1)}, u32[]{:S(2)}, u32[]{:S(2)}) collective-permute-start(bf16[128,3072]{1,0:T(8,128)(2,1)} %get-tuple-element.585), channel_id=1, source_target_pairs={{0,1},{1,2},{2,3},{3,4},{4,5},{5,6},{6,7},{7,8},{8,9},{9,10},{10,1... | collective-permute-start | bytes 2359304 | tf_op jit(solution)/shard_map/while/body/eval_jaxpr/ppermute | solution.py:20
  926.8 6.0 slice-start
  930.1 2.7 slice-start.1
  936.2 18.1 %collective-permute-start.1 = (bf16[128,1536]{1,0:T(8,128)(2,1)}, bf16[128,1536]{1,0:T(8,128)(2,1)S(1)}, u32[]{:S(2)}, u32[]{:S(2)}) collective-permute-start(bf16[128,1536]{1,0:T(8,128)(2,1)} %get-tuple-element.587), channel_id=1, source_target_pairs={{0,32},{32,64},{64,96},{96,128},{128,160},{160,192},{192,224},{1,3... | collective-permute-start | bytes 1179656 | tf_op jit(solution)/shard_map/while/body/eval_jaxpr/ppermute | solution.py:26
  974.5 18.3 %collective-permute-start = (bf16[128,3072]{1,0:T(8,128)(2,1)}, bf16[128,3072]{1,0:T(8,128)(2,1)S(1)}, u32[]{:S(2)}, u32[]{:S(2)}) collective-permute-start(bf16[128,3072]{1,0:T(8,128)(2,1)} %get-tuple-element.585), channel_id=1, source_target_pairs={{0,1},{1,2},{2,3},{3,4},{4,5},{5,6},{6,7},{7,8},{8,9},{9,10},{10,1... | collective-permute-start | bytes 2359304 | tf_op jit(solution)/shard_map/while/body/eval_jaxpr/ppermute | solution.py:20
  1010.1 6.0 slice-start
  1013.5 2.7 slice-start.1
  1019.5 3.8 collective-permute-start.1
Sparse Core Ops, SparseCore 0:
  11.2 102.6 all-gather.6
  116.4 125.1 all-gather.4
where the time goes:
time: 1030 us
  waiting for transfers between devices  668 us (65%)
  other arithmetic  126 us (12%)
  local copies, waits for them, and re-layouts  103 us (10%)
  matrix products  82.5 us (8%)
  loops' own time  20.9 us (2%)
  starting transfers between devices  15.9 us (2%)
  between operations  14.1 us (1%)
    ppermute x11, waiting for transfers between devices, shifted_2(): return lax.ppermute(x, axis, pairs)  286 us
    ppermute x12, waiting for transfers between devices, shifted(): return lax.ppermute(value, axis, pairs)  255 us
    all_gather x1, waiting for transfers between devices, on_device(): lax.all_gather(w_qkv[0], 'blk', axis=0, tiled=True)  126 us
    dot_general x4, matrix products, project(): qkv = jnp.dot(modulated, full_qkv, preferred_element_type=jnp.float32)  28.6 us
    dot_general x11, matrix products, slot_step(): jnp.dot(one_hot, modulation_table, precision=lax.Precision.HIGHEST)  26.6 us
    select_n x11, other arithmetic, slot_step(): jnp.where(active, lax.dynamic_update_index_in_dim(own_store, fresh_kv, pa...  25.1 us
    select_n x11, other arithmetic, slot_step(): jnp.where(active, lax.dynamic_update_index_in_dim(near_store, near_fresh,...  24.3 us
    concatenate x4, other arithmetic, attend(): jnp.concatenate([own_rows.reshape(-1, 2 * inner_width), near_rows.reshape...  22.5 us
  transfers between devices with their start and end apart: 25, of which 24 were waited for; matrix products, arithmetic and copies ran while one was open for 5% of the time, Pallas kernels for 0%

commit v1 on v0

--- a/solution.py
+++ b/solution.py
@@ -47,7 +47,9 @@
     sections = lax.axis_size("section")
     section_id = lax.axis_index("section")
     full_qkv, full_out = (
-        lax.all_gather(w_qkv[0], "blk", axis=0, tiled=True),
+        jnp.concatenate(
+            lax.all_to_all(jnp.stack([w_qkv[0]] * lax.axis_size("blk")), "blk", 0, 0), axis=0
+        ),
         lax.all_gather(w_out[0], "blk", axis=0, tiled=True),
     )
     query_gain = q_gain[0]

time: 1030 us -> 1240 us (1.20)
  waiting for transfers between devices: 668 us -> 843 us
  starting transfers between devices: 15.9 us -> 33.6 us
    ppermute x12, waiting for transfers between devices: 255 us -> 553 us  [shifted(): return lax.ppermute(value, axis, pairs)]
    all_gather x1 -> x0, waiting for transfers between devices: 126 us -> none  [on_device(): lax.all_gather(w_qkv[0], 'blk', axis=0, tiled=True)]
  transfers between devices with their start and end apart: 25 -> 25, of which waited for: 24 -> 23; matrix products, arithmetic and copies ran while one was open for 5% -> 4% of each run, Pallas kernels for 0% -> 0%
where the time goes in v1:
time: 1240 us; the launch traced here: 1230 us
  waiting for transfers between devices  843 us (68%)
  other arithmetic  126 us (10%)
  local copies, waits for them, and re-layouts  110 us (9%)
  matrix products  82.8 us (7%)
  starting transfers between devices  33.6 us (3%)
  loops' own time  23.8 us (2%)
  between operations  14.1 us (1%)
    ppermute x12, waiting for transfers between devices, shifted(): return lax.ppermute(value, axis, pairs)  553 us
    ppermute x11, waiting for transfers between devices, shifted_2(): return lax.ppermute(x, axis, pairs)  289 us
    dot_general x4, matrix products, project(): qkv = jnp.dot(modulated, full_qkv, preferred_element_type=jnp.float32)  28.6 us
    dot_general x11, matrix products, slot_step(): jnp.dot(one_hot, modulation_table, precision=lax.Precision.HIGHEST)  26.8 us
    select_n x11, other arithmetic, slot_step(): jnp.where(active, lax.dynamic_update_index_in_dim(own_store, fresh_kv, pa...  25.1 us
  transfers between devices with their start and end apart: 25, of which 23 were waited for; matrix products, arithmetic and copies ran while one was open for 4% of the time, Pallas kernels for 0%

profile of v1, /device:TPU:7, one launch (start us, length us, event | category | flops | bytes accessed | tf_op | source)
XLA Modules:
  0.0 1233.1 jit_solution(15838335971762245686)
XLA Ops:
  7.2 3.8 copy.63
  11.0 6.7 stack.3
  17.7 11.5 all-to-all-start
  32.2 406.2 %collective-permute-done.2 = bf16[4,128,3072]{2,1,0:T(8,128)(2,1)} collective-permute-done((bf16[4,128,3072]{2,1,0:T(8,128)(2,1)}, bf16[4,128,3072]{2,1,0:T(8,128)(2,1)}, u32[]{:S(2)}, u32[]{:S(2)}) %collective-permute-start.2) | collective-permute-done | bytes 3145760 | tf_op jit(solution)/shard_map/ppermute | solution.py:20
  439.7 786.5 %while.20 = (s32[]{:T(128)}, bf16[128,1536]{1,0:T(8,128)(2,1)S(1)}, bf16[4,128,3072]{2,1,0:T(8,128)(2,1)}, bf16[4,128,3072]{2,1,0:T(8,128)(2,1)}, bf16[4,128,153...) while((s32[]{:T(128)}, bf16[128,1536]{1,0:T(8,128)(2,1)S(1)}, ...), condition=%wide.region_11.12_spmd, body=%wide.region_0.11_spmd.sunk | while | flops 3260855808 | bytes 107183792 | solution.py:162
  451.9 18.9 %collective-permute-done = bf16[128,3072]{1,0:T(8,128)(2,1)S(1)} collective-permute-done((bf16[128,3072]{1,0:T(8,128)(2,1)}, bf16[128,3072]{1,0:T(8,128)(2,1)S(1)}, u32[]{:S(2)}, u32[]{:S(2)}) %collective-permute-start) | collective-permute-done | bytes 786464 | tf_op jit(solution)/shard_map/while/body/eval_jaxpr/ppermute | solution.py:20
  490.0 6.8 collective-permute-start
  499.0 7.1 collective-permute-done
  513.0 14.5 %collective-permute-done.1 = bf16[128,1536]{1,0:T(8,128)(2,1)S(1)} collective-permute-done((bf16[128,1536]{1,0:T(8,128)(2,1)}, bf16[128,1536]{1,0:T(8,128)(2,1)S(1)}, u32[]{:S(2)}, u32[]{:S(2)}) %collective-permute-start.1) | collective-permute-done | bytes 393248 | tf_op jit(solution)/shard_map/while/body/eval_jaxpr/ppermute | solution.py:26
  539.4 14.2 %collective-permute-done = bf16[128,3072]{1,0:T(8,128)(2,1)S(1)} collective-permute-done((bf16[128,3072]{1,0:T(8,128)(2,1)}, bf16[128,3072]{1,0:T(8,128)(2,1)S(1)}, u32[]{:S(2)}, u32[]{:S(2)}) %collective-permute-start) | collective-permute-done | bytes 786464 | tf_op jit(solution)/shard_map/while/body/eval_jaxpr/ppermute | solution.py:20
  560.4 7.3 collective-permute-done.1
  579.7 14.4 %collective-permute-done = bf16[128,3072]{1,0:T(8,128)(2,1)S(1)} collective-permute-done((bf16[128,3072]{1,0:T(8,128)(2,1)}, bf16[128,3072]{1,0:T(8,128)(2,1)S(1)}, u32[]{:S(2)}, u32[]{:S(2)}) %collective-permute-start) | collective-permute-done | bytes 786464 | tf_op jit(solution)/shard_map/while/body/eval_jaxpr/ppermute | solution.py:20
  601.0 7.1 collective-permute-done.1
  620.0 14.4 %collective-permute-done = bf16[128,3072]{1,0:T(8,128)(2,1)S(1)} collective-permute-done((bf16[128,3072]{1,0:T(8,128)(2,1)}, bf16[128,3072]{1,0:T(8,128)(2,1)S(1)}, u32[]{:S(2)}, u32[]{:S(2)}) %collective-permute-start) | collective-permute-done | bytes 786464 | tf_op jit(solution)/shard_map/while/body/eval_jaxpr/ppermute | solution.py:20
  641.3 7.1 collective-permute-done.1
  660.3 14.4 %collective-permute-done = bf16[128,3072]{1,0:T(8,128)(2,1)S(1)} collective-permute-done((bf16[128,3072]{1,0:T(8,128)(2,1)}, bf16[128,3072]{1,0:T(8,128)(2,1)S(1)}, u32[]{:S(2)}, u32[]{:S(2)}) %collective-permute-start) | collective-permute-done | bytes 786464 | tf_op jit(solution)/shard_map/while/body/eval_jaxpr/ppermute | solution.py:20
  681.6 7.1 collective-permute-done.1
  700.7 12.2 collective-permute-done
  719.8 205.2 %collective-permute-done.1 = bf16[128,1536]{1,0:T(8,128)(2,1)S(1)} collective-permute-done((bf16[128,1536]{1,0:T(8,128)(2,1)}, bf16[128,1536]{1,0:T(8,128)(2,1)S(1)}, u32[]{:S(2)}, u32[]{:S(2)}) %collective-permute-start.1) | collective-permute-done | bytes 393248 | tf_op jit(solution)/shard_map/while/body/eval_jaxpr/ppermute | solution.py:26
  931.8 13.7 %conditional.4 = (bf16[128,12,128]{0,2,1:T(8,128)(2,1)}, bf16[128,3072]{1,0:T(8,128)(2,1)}, bf16[1,128,3072]{2,1,0:T(8,128)(2,1)}) conditional(s32[]{:T(128)} %convert_element_type.92, () %tuple.70, (bf16[128,1536]{1,0:T(8,128)(2,1)S(1)}, f32[4608]{0:T(1024)}, bf16[1536,4608]{1,0:T(8,128)(2,1)}, f32[1,128]{1,0:T(1,128)S(1)}) %tuple.71), branch_computations={%region_2.2_spmd, %region_3.6_spmd} | conditional | flops 1815284864 | bytes 26018840 | solution.py:105
  933.0 7.2 fusion.6
  948.0 11.9 collective-permute-done
  962.1 24.4 %conditional.5 = (bf16[128,1536]{1,0:T(8,128)(2,1)}, bf16[1,128,1536]{2,1,0:T(8,128)(2,1)}) conditional(s32[]{:T(128)} %convert_element_type.92, () %tuple.69, (bf16[128,1536]{1,0:T(8,128)(2,1)S(1)}, f32[4608]{0:T(1024)}, bf16[4,128,3072]{2,1,0:T(8,128)(2,1)}, bf16[4,128,3072]{2,1,0:T(8,128)(2,1)}, f32[1,128]{1,0:T(1,128)S(1)}, ...), branch_computations={%region_7.7_spmd, %region_8.10_spmd} | conditional | flops 1443506688 | bytes 69053088 | solution.py:152
  965.3 4.7 copy.31
  970.0 5.6 pad_maximum_fusion
  977.2 3.3 bitcast_reduce_fusion
  989.8 10.3 collective-permute-done.1
  1007.0 13.7 %conditional.4 = (bf16[128,12,128]{0,2,1:T(8,128)(2,1)}, bf16[128,3072]{1,0:T(8,128)(2,1)}, bf16[1,128,3072]{2,1,0:T(8,128)(2,1)}) conditional(s32[]{:T(128)} %convert_element_type.92, () %tuple.70, (bf16[128,1536]{1,0:T(8,128)(2,1)S(1)}, f32[4608]{0:T(1024)}, bf16[1536,4608]{1,0:T(8,128)(2,1)}, f32[1,128]{1,0:T(1,128)S(1)}) %tuple.71), branch_computations={%region_2.2_spmd, %region_3.6_spmd} | conditional | flops 1815284864 | bytes 26018840 | solution.py:105
  1008.2 7.1 fusion.6
  1023.1 11.9 collective-permute-done
  1037.3 24.4 %conditional.5 = (bf16[128,1536]{1,0:T(8,128)(2,1)}, bf16[1,128,1536]{2,1,0:T(8,128)(2,1)}) conditional(s32[]{:T(128)} %convert_element_type.92, () %tuple.69, (bf16[128,1536]{1,0:T(8,128)(2,1)S(1)}, f32[4608]{0:T(1024)}, bf16[4,128,3072]{2,1,0:T(8,128)(2,1)}, bf16[4,128,3072]{2,1,0:T(8,128)(2,1)}, f32[1,128]{1,0:T(1,128)S(1)}, ...), branch_computations={%region_7.7_spmd, %region_8.10_spmd} | conditional | flops 1443506688 | bytes 69053088 | solution.py:152
  1040.5 4.7 copy.31
  1045.2 5.6 pad_maximum_fusion
  1052.3 3.3 bitcast_reduce_fusion
  1064.9 12.3 collective-permute-done.1
  1084.1 13.7 %conditional.4 = (bf16[128,12,128]{0,2,1:T(8,128)(2,1)}, bf16[128,3072]{1,0:T(8,128)(2,1)}, bf16[1,128,3072]{2,1,0:T(8,128)(2,1)}) conditional(s32[]{:T(128)} %convert_element_type.92, () %tuple.70, (bf16[128,1536]{1,0:T(8,128)(2,1)S(1)}, f32[4608]{0:T(1024)}, bf16[1536,4608]{1,0:T(8,128)(2,1)}, f32[1,128]{1,0:T(1,128)S(1)}) %tuple.71), branch_computations={%region_2.2_spmd, %region_3.6_spmd} | conditional | flops 1815284864 | bytes 26018840 | solution.py:105
  1085.3 7.1 fusion.6
  1100.2 11.9 collective-permute-done
  1114.4 24.4 %conditional.5 = (bf16[128,1536]{1,0:T(8,128)(2,1)}, bf16[1,128,1536]{2,1,0:T(8,128)(2,1)}) conditional(s32[]{:T(128)} %convert_element_type.92, () %tuple.69, (bf16[128,1536]{1,0:T(8,128)(2,1)S(1)}, f32[4608]{0:T(1024)}, bf16[4,128,3072]{2,1,0:T(8,128)(2,1)}, bf16[4,128,3072]{2,1,0:T(8,128)(2,1)}, f32[1,128]{1,0:T(1,128)S(1)}, ...), branch_computations={%region_7.7_spmd, %region_8.10_spmd} | conditional | flops 1443506688 | bytes 69053088 | solution.py:152
  1117.6 4.7 copy.31
  1122.3 5.6 pad_maximum_fusion
  1142.0 14.9 %collective-permute-done.1 = bf16[128,1536]{1,0:T(8,128)(2,1)S(1)} collective-permute-done((bf16[128,1536]{1,0:T(8,128)(2,1)}, bf16[128,1536]{1,0:T(8,128)(2,1)S(1)}, u32[]{:S(2)}, u32[]{:S(2)}) %collective-permute-start.1) | collective-permute-done | bytes 393248 | tf_op jit(solution)/shard_map/while/body/eval_jaxpr/ppermute | solution.py:26
  1163.8 13.7 %conditional.4 = (bf16[128,12,128]{0,2,1:T(8,128)(2,1)}, bf16[128,3072]{1,0:T(8,128)(2,1)}, bf16[1,128,3072]{2,1,0:T(8,128)(2,1)}) conditional(s32[]{:T(128)} %convert_element_type.92, () %tuple.70, (bf16[128,1536]{1,0:T(8,128)(2,1)S(1)}, f32[4608]{0:T(1024)}, bf16[1536,4608]{1,0:T(8,128)(2,1)}, f32[1,128]{1,0:T(1,128)S(1)}) %tuple.71), branch_computations={%region_2.2_spmd, %region_3.6_spmd} | conditional | flops 1815284864 | bytes 26018840 | solution.py:105
  1165.0 7.1 fusion.6
  1179.9 15.9 %collective-permute-done = bf16[128,3072]{1,0:T(8,128)(2,1)S(1)} collective-permute-done((bf16[128,3072]{1,0:T(8,128)(2,1)}, bf16[128,3072]{1,0:T(8,128)(2,1)S(1)}, u32[]{:S(2)}, u32[]{:S(2)}) %collective-permute-start) | collective-permute-done | bytes 786464 | tf_op jit(solution)/shard_map/while/body/eval_jaxpr/ppermute | solution.py:20
  1198.1 24.4 %conditional.5 = (bf16[128,1536]{1,0:T(8,128)(2,1)}, bf16[1,128,1536]{2,1,0:T(8,128)(2,1)}) conditional(s32[]{:T(128)} %convert_element_type.92, () %tuple.69, (bf16[128,1536]{1,0:T(8,128)(2,1)S(1)}, f32[4608]{0:T(1024)}, bf16[4,128,3072]{2,1,0:T(8,128)(2,1)}, bf16[4,128,3072]{2,1,0:T(8,128)(2,1)}, f32[1,128]{1,0:T(1,128)S(1)}, ...), branch_computations={%region_7.7_spmd, %region_8.10_spmd} | conditional | flops 1443506688 | bytes 69053088 | solution.py:152
  1201.2 4.7 copy.31
  1205.9 5.6 pad_maximum_fusion
  (276 shorter events, 281.7 us)
Async XLA Ops:
  7.2 3.8 copy-start
  17.7 13.5 %copy-start.1 = (f32[1,16,3,1536]{3,1,2,0:T(8,128)S(1)}, f32[1,16,3,1536]{3,1,2,0:T(8,128)}, u32[]{:S(2)}) copy-start(f32[1,16,3,1536]{3,1,2,0:T(8,128)} %param.22) | copy-start | bytes 884740
  17.7 420.7 %all-to-all-start = ((bf16[32,48,4608]{2,1,0:T(8,128)(2,1)}), bf16[32,48,4608]{2,1,0:T(8,128)(2,1)}, u32[]{:S(2)}, u32[]{:S(2)}) async-start(bf16[32,48,4608]{2,1,0:T(8,128)(2,1)} %stack.3), calls=%async_computation | async-start | bytes 28311552 | tf_op jit(solution)/shard_map/all_to_all | solution.py:51
  29.2 410.6 %copy-start.2 = (f32[1,128]{1,0:T(1,128)S(1)}, f32[1,128]{1,0:T(1,128)}, u32[]{:S(2)}) copy-start(f32[1,128]{1,0:T(1,128)} %param.20) | copy-start | bytes 1540
  29.2 410.6 %copy-start.3 = (s32[4]{0:T(128)S(1)}, s32[4]{0:T(128)}, u32[]{:S(2)}) copy-start(s32[4]{0:T(128)} %param.25) | copy-start | bytes 52
  29.2 410.5 %copy-start.4 = (s32[4]{0:T(128)S(1)}, s32[4]{0:T(128)}, u32[]{:S(2)}) copy-start(s32[4]{0:T(128)} %param.24) | copy-start | bytes 52
  29.2 410.5 %copy-start.5 = (f32[1,128]{1,0:T(1,128)S(1)}, f32[1,128]{1,0:T(1,128)}, u32[]{:S(2)}) copy-start(f32[1,128]{1,0:T(1,128)} %param.21) | copy-start | bytes 1540
  29.2 409.2 %all-gather.3.cloned.1.call-start = ((), (), s32[]{:S(2)}) async-start(), calls=%async_computation.1 | async-start | bytes 4866048 | tf_op jit(solution)/shard_map/all_gather | solution.py:53
  29.9 408.5 %collective-permute-start.2 = (bf16[4,128,3072]{2,1,0:T(8,128)(2,1)}, bf16[4,128,3072]{2,1,0:T(8,128)(2,1)}, u32[]{:S(2)}, u32[]{:S(2)}) collective-permute-start(bf16[4,128,3072]{2,1,0:T(8,128)(2,1)} %bitcast.20), channel_id=1, source_target_pairs={{0,1},{1,2},{2,3},{3,4},{4,5},{5,6},{6,7},{7,8},{8,9},{9,10},{10,1... | collective-permute-start | bytes 9437192 | tf_op jit(solution)/shard_map/ppermute | solution.py:20
  449.7 21.1 %collective-permute-start = (bf16[128,3072]{1,0:T(8,128)(2,1)}, bf16[128,3072]{1,0:T(8,128)(2,1)S(1)}, u32[]{:S(2)}, u32[]{:S(2)}) collective-permute-start(bf16[128,3072]{1,0:T(8,128)(2,1)} %get-tuple-element.585), channel_id=1, source_target_pairs={{0,1},{1,2},{2,3},{3,4},{4,5},{5,6},{6,7},{7,8},{8,9},{9,10},{10,1... | collective-permute-start | bytes 2359304 | tf_op jit(solution)/shard_map/while/body/eval_jaxpr/ppermute | solution.py:20
  474.6 5.7 collective-permute-start.1
  490.0 16.0 %collective-permute-start = (bf16[128,3072]{1,0:T(8,128)(2,1)}, bf16[128,3072]{1,0:T(8,128)(2,1)S(1)}, u32[]{:S(2)}, u32[]{:S(2)}) collective-permute-start(bf16[128,3072]{1,0:T(8,128)(2,1)} %get-tuple-element.585), channel_id=1, source_target_pairs={{0,1},{1,2},{2,3},{3,4},{4,5},{5,6},{6,7},{7,8},{8,9},{9,10},{10,1... | collective-permute-start | bytes 2359304 | tf_op jit(solution)/shard_map/while/body/eval_jaxpr/ppermute | solution.py:20
  509.8 17.6 %collective-permute-start.1 = (bf16[128,1536]{1,0:T(8,128)(2,1)}, bf16[128,1536]{1,0:T(8,128)(2,1)S(1)}, u32[]{:S(2)}, u32[]{:S(2)}) collective-permute-start(bf16[128,1536]{1,0:T(8,128)(2,1)} %get-tuple-element.587), channel_id=1, source_target_pairs={{0,32},{32,64},{64,96},{96,128},{128,160},{160,192},{192,224},{1,3... | collective-permute-start | bytes 1179656 | tf_op jit(solution)/shard_map/while/body/eval_jaxpr/ppermute | solution.py:26
  537.2 16.4 %collective-permute-start = (bf16[128,3072]{1,0:T(8,128)(2,1)}, bf16[128,3072]{1,0:T(8,128)(2,1)S(1)}, u32[]{:S(2)}, u32[]{:S(2)}) collective-permute-start(bf16[128,3072]{1,0:T(8,128)(2,1)} %get-tuple-element.585), channel_id=1, source_target_pairs={{0,1},{1,2},{2,3},{3,4},{4,5},{5,6},{6,7},{7,8},{8,9},{9,10},{10,1... | collective-permute-start | bytes 2359304 | tf_op jit(solution)/shard_map/while/body/eval_jaxpr/ppermute | solution.py:20
  557.3 10.4 collective-permute-start.1
  577.5 16.6 %collective-permute-start = (bf16[128,3072]{1,0:T(8,128)(2,1)}, bf16[128,3072]{1,0:T(8,128)(2,1)S(1)}, u32[]{:S(2)}, u32[]{:S(2)}) collective-permute-start(bf16[128,3072]{1,0:T(8,128)(2,1)} %get-tuple-element.585), channel_id=1, source_target_pairs={{0,1},{1,2},{2,3},{3,4},{4,5},{5,6},{6,7},{7,8},{8,9},{9,10},{10,1... | collective-permute-start | bytes 2359304 | tf_op jit(solution)/shard_map/while/body/eval_jaxpr/ppermute | solution.py:20
  597.9 10.2 collective-permute-start.1
  617.8 16.6 %collective-permute-start = (bf16[128,3072]{1,0:T(8,128)(2,1)}, bf16[128,3072]{1,0:T(8,128)(2,1)S(1)}, u32[]{:S(2)}, u32[]{:S(2)}) collective-permute-start(bf16[128,3072]{1,0:T(8,128)(2,1)} %get-tuple-element.585), channel_id=1, source_target_pairs={{0,1},{1,2},{2,3},{3,4},{4,5},{5,6},{6,7},{7,8},{8,9},{9,10},{10,1... | collective-permute-start | bytes 2359304 | tf_op jit(solution)/shard_map/while/body/eval_jaxpr/ppermute | solution.py:20
  638.2 10.2 collective-permute-start.1
  658.1 16.6 %collective-permute-start = (bf16[128,3072]{1,0:T(8,128)(2,1)}, bf16[128,3072]{1,0:T(8,128)(2,1)S(1)}, u32[]{:S(2)}, u32[]{:S(2)}) collective-permute-start(bf16[128,3072]{1,0:T(8,128)(2,1)} %get-tuple-element.585), channel_id=1, source_target_pairs={{0,1},{1,2},{2,3},{3,4},{4,5},{5,6},{6,7},{7,8},{8,9},{9,10},{10,1... | collective-permute-start | bytes 2359304 | tf_op jit(solution)/shard_map/while/body/eval_jaxpr/ppermute | solution.py:20
  678.5 10.2 collective-permute-start.1
  698.5 14.4 %collective-permute-start = (bf16[128,3072]{1,0:T(8,128)(2,1)}, bf16[128,3072]{1,0:T(8,128)(2,1)S(1)}, u32[]{:S(2)}, u32[]{:S(2)}) collective-permute-start(bf16[128,3072]{1,0:T(8,128)(2,1)} %get-tuple-element.585), channel_id=1, source_target_pairs={{0,1},{1,2},{2,3},{3,4},{4,5},{5,6},{6,7},{7,8},{8,9},{9,10},{10,1... | collective-permute-start | bytes 2359304 | tf_op jit(solution)/shard_map/while/body/eval_jaxpr/ppermute | solution.py:20
  716.6 208.3 %collective-permute-start.1 = (bf16[128,1536]{1,0:T(8,128)(2,1)}, bf16[128,1536]{1,0:T(8,128)(2,1)S(1)}, u32[]{:S(2)}, u32[]{:S(2)}) collective-permute-start(bf16[128,1536]{1,0:T(8,128)(2,1)} %get-tuple-element.587), channel_id=1, source_target_pairs={{0,32},{32,64},{64,96},{96,128},{128,160},{160,192},{192,224},{1,3... | collective-permute-start | bytes 1179656 | tf_op jit(solution)/shard_map/while/body/eval_jaxpr/ppermute | solution.py:26
  945.5 14.4 %collective-permute-start = (bf16[128,3072]{1,0:T(8,128)(2,1)}, bf16[128,3072]{1,0:T(8,128)(2,1)S(1)}, u32[]{:S(2)}, u32[]{:S(2)}) collective-permute-start(bf16[128,3072]{1,0:T(8,128)(2,1)} %get-tuple-element.585), channel_id=1, source_target_pairs={{0,1},{1,2},{2,3},{3,4},{4,5},{5,6},{6,7},{7,8},{8,9},{9,10},{10,1... | collective-permute-start | bytes 2359304 | tf_op jit(solution)/shard_map/while/body/eval_jaxpr/ppermute | solution.py:20
  977.2 6.0 slice-start
  980.5 2.7 slice-start.1
  986.5 13.5 %collective-permute-start.1 = (bf16[128,1536]{1,0:T(8,128)(2,1)}, bf16[128,1536]{1,0:T(8,128)(2,1)S(1)}, u32[]{:S(2)}, u32[]{:S(2)}) collective-permute-start(bf16[128,1536]{1,0:T(8,128)(2,1)} %get-tuple-element.587), channel_id=1, source_target_pairs={{0,32},{32,64},{64,96},{96,128},{128,160},{160,192},{192,224},{1,3... | collective-permute-start | bytes 1179656 | tf_op jit(solution)/shard_map/while/body/eval_jaxpr/ppermute | solution.py:26
  1020.7 14.4 %collective-permute-start = (bf16[128,3072]{1,0:T(8,128)(2,1)}, bf16[128,3072]{1,0:T(8,128)(2,1)S(1)}, u32[]{:S(2)}, u32[]{:S(2)}) collective-permute-start(bf16[128,3072]{1,0:T(8,128)(2,1)} %get-tuple-element.585), channel_id=1, source_target_pairs={{0,1},{1,2},{2,3},{3,4},{4,5},{5,6},{6,7},{7,8},{8,9},{9,10},{10,1... | collective-permute-start | bytes 2359304 | tf_op jit(solution)/shard_map/while/body/eval_jaxpr/ppermute | solution.py:20
  1052.3 6.0 slice-start
  1055.6 2.7 slice-start.1
  1061.7 15.5 %collective-permute-start.1 = (bf16[128,1536]{1,0:T(8,128)(2,1)}, bf16[128,1536]{1,0:T(8,128)(2,1)S(1)}, u32[]{:S(2)}, u32[]{:S(2)}) collective-permute-start(bf16[128,1536]{1,0:T(8,128)(2,1)} %get-tuple-element.587), channel_id=1, source_target_pairs={{0,32},{32,64},{64,96},{96,128},{128,160},{160,192},{192,224},{1,3... | collective-permute-start | bytes 1179656 | tf_op jit(solution)/shard_map/while/body/eval_jaxpr/ppermute | solution.py:26
  1097.8 14.4 %collective-permute-start = (bf16[128,3072]{1,0:T(8,128)(2,1)}, bf16[128,3072]{1,0:T(8,128)(2,1)S(1)}, u32[]{:S(2)}, u32[]{:S(2)}) collective-permute-start(bf16[128,3072]{1,0:T(8,128)(2,1)} %get-tuple-element.585), channel_id=1, source_target_pairs={{0,1},{1,2},{2,3},{3,4},{4,5},{5,6},{6,7},{7,8},{8,9},{9,10},{10,1... | collective-permute-start | bytes 2359304 | tf_op jit(solution)/shard_map/while/body/eval_jaxpr/ppermute | solution.py:20
  1129.4 6.0 slice-start
  1132.7 2.7 slice-start.1
  1138.8 18.1 %collective-permute-start.1 = (bf16[128,1536]{1,0:T(8,128)(2,1)}, bf16[128,1536]{1,0:T(8,128)(2,1)S(1)}, u32[]{:S(2)}, u32[]{:S(2)}) collective-permute-start(bf16[128,1536]{1,0:T(8,128)(2,1)} %get-tuple-element.587), channel_id=1, source_target_pairs={{0,32},{32,64},{64,96},{96,128},{128,160},{160,192},{192,224},{1,3... | collective-permute-start | bytes 1179656 | tf_op jit(solution)/shard_map/while/body/eval_jaxpr/ppermute | solution.py:26
  1177.5 18.3 %collective-permute-start = (bf16[128,3072]{1,0:T(8,128)(2,1)}, bf16[128,3072]{1,0:T(8,128)(2,1)S(1)}, u32[]{:S(2)}, u32[]{:S(2)}) collective-permute-start(bf16[128,3072]{1,0:T(8,128)(2,1)} %get-tuple-element.585), channel_id=1, source_target_pairs={{0,1},{1,2},{2,3},{3,4},{4,5},{5,6},{6,7},{7,8},{8,9},{9,10},{10,1... | collective-permute-start | bytes 2359304 | tf_op jit(solution)/shard_map/while/body/eval_jaxpr/ppermute | solution.py:20
  1213.1 6.0 slice-start
  1216.4 2.7 slice-start.1
  1222.5 3.8 collective-permute-start.1
Sparse Core Ops, SparseCore 0:
  32.6 156.9 all-gather.2
